TPU v7x, 32 devices: a whole 2x2x4 slice. The times are simulated.
32 devices in a mesh: wide: 8 (over z, y), narrow: 4 (over x, core).
Axes of the slice: x: 2, y: 2, z: 4, core: 2. Of those that a mesh axis runs over, the one named last changes fastest.
Arguments:
- tokens: bfloat16 [80, 1024, 768], P('wide', 'narrow'), may hold values from -12 to 12, as said below
- usable: int32 [80, 1024], P('wide', 'narrow'), may hold values from 0 to 1, as said below
- conv_weight: bfloat16 [2304, 384], P(('wide', 'narrow')), may hold values from -0.125 to 0.125
- point_weight: bfloat16 [768, 384], P(('wide', 'narrow')), may hold values from -0.3125 to 0.3125
- head_weight: bfloat16 [768, 5313], P(('wide', 'narrow')), may hold values from -0.21875 to 0.21875
- first_gain: float32 [768], replicated, may hold values from 0.1 to 1.9
- first_shift: float32 [768], replicated, may hold values from -3 to 3
- second_gain: float32 [384], replicated, may hold values from 0.1 to 1.9
- second_shift: float32 [384], replicated, may hold values from -3 to 3
- point_bias: float32 [768], replicated, may hold values from -2 to 2
- head_bias: float32 [5313], replicated, may hold values from -1 to 1
- cot_block: bfloat16 [80, 1024, 768], P('wide', 'narrow'), may hold values from -6 to 6
- cot_tracks: bfloat16 [80, 5313, 1024], P('wide', None, 'narrow'), may hold values from -6 to 6
Outputs:
- block_out: bfloat16 [80, 1024, 768], P('wide', 'narrow')
- tracks_out: bfloat16 [80, 5313, 1024], P('wide', None, 'narrow')
- grad_tokens: float32 [80, 1024, 768], P('wide', 'narrow')
- grad_conv: float32 [2304, 384], P(('wide', 'narrow'))
- grad_point: float32 [768, 384], P(('wide', 'narrow'))
- grad_head: float32 [768, 5313], P(('wide', 'narrow'))
- grad_first_gain: float32 [768], replicated
- grad_first_shift: float32 [768], replicated
- grad_second_gain: float32 [384], replicated
- grad_second_shift: float32 [384], replicated
- grad_point_bias: float32 [768], replicated
- grad_head_bias: float32 [5313], replicated
Inputs may be any that keep to these rules, and one draw needn't show every extreme that they name: 1 marks a usable bin. Blacklisted runs of 16 aligned bins and scattered unmappable bins are 0, with a blacklist rate that differs from window to window; the first bin of every window is usable. `tokens`: activations of order one whose scale grows along the bins and windows.
All inputs are finite; a program needn't handle non-finite values.
Results may differ from a plain program's by a relative error of at most 0.008.
Values may be sent and summed in bfloat16 or wider, within the bound.
No kernel may reach another device: no remote copies, remote signals or barrier semaphores. Data moves between devices by JAX's collectives and lax.ppermute only.
A program may use at most 256 MiB of HBM per device.

v0:
```python
import jax
import jax.numpy as jnp
from jax import lax
from jax.sharding import PartitionSpec as P

DILATION_STEP = 11


epsilon = 1e-05


def with_halo(shard, sides, width):
    for axis, dim in sides:
        count, length = (lax.axis_size(axis), shard.shape[dim])
        up = [(i, (i + 1) % count) for i in range(count - 1)]
        down = [(j, i) for i, j in up]
        last = lax.slice_in_dim(shard, length - width, length, axis=dim)
        first = lax.slice_in_dim(shard, 0, width, axis=dim)
        before = lax.ppermute(last, axis, up)
        after = lax.ppermute(first, axis, down)
        shard = jnp.concatenate([before, shard, after], axis=dim)
    return shard


def norm_stats(values, weight):
    totals, counted = lax.psum(
        (jnp.sum(values * weight, axis=(0, 1)), jnp.sum(weight)), ("wide", "narrow")
    )
    mean_value = totals / counted
    centred = values - mean_value
    spread = lax.psum(jnp.sum(weight * centred * centred, axis=(0, 1)), ("wide", "narrow"))
    variance = spread / counted
    return (mean_value, lax.rsqrt(variance + epsilon), counted)


def convolve(padded_input, convolution_kernel, local_bin_count):
    hidden_state = jnp.einsum(
        "ldo,ov->ldv",
        padded_input[:, 0:local_bin_count],
        convolution_kernel[0],
        preferred_element_type=jnp.float32,
    )
    for kernel_position in range(1, 3):
        hidden_state = hidden_state + jnp.einsum(
            "ldo,ov->ldv",
            padded_input[
                :,
                kernel_position * DILATION_STEP : kernel_position * DILATION_STEP + local_bin_count,
            ],
            convolution_kernel[kernel_position],
            preferred_element_type=jnp.float32,
        )
    return hidden_state


def gelu_back(preact, upstream):
    return jax.vjp(jax.nn.gelu, preact)[1](upstream)[0]


def norm_back(grad_inner, normed, scale_inv, gain, grad_gain, grad_shift, weight, counted):
    grad_normed = grad_inner * gain
    return scale_inv * (
        grad_normed - weight / counted * (gain * grad_shift + normed * gain * grad_gain)
    )


def shards(
    tokens,
    usable,
    conv_weight,
    point_weight,
    head_weight,
    first_gain,
    first_shift,
    second_gain,
    second_shift,
    point_bias,
    head_bias,
    cot_block,
    cot_tracks,
):
    local_bin_count = tokens.shape[1]
    weight = usable.astype(jnp.float32)[:, :, None]
    row_weight = usable.astype(jnp.float32)[:, None, :]
    source = tokens.astype(jnp.float32)
    conv_full, point_full = (
        lax.all_gather(conv_weight, ("wide", "narrow"), axis=0, tiled=True),
        lax.all_gather(point_weight, ("wide", "narrow"), axis=0, tiled=True),
    )
    first_mean, first_scale, counted = norm_stats(source, weight)
    first_normed = (source - first_mean) * first_scale
    first_inner = first_normed * first_gain + first_shift
    first_activated = jax.nn.gelu(first_inner).astype(jnp.bfloat16)
    padded_input = with_halo(first_activated, (("narrow", 1),), DILATION_STEP)
    convolution_kernel = conv_full.reshape(3, -1, conv_full.shape[1])
    hidden_state = convolve(padded_input, convolution_kernel, local_bin_count)
    second_mean, second_scale, counted_two = norm_stats(hidden_state, weight)
    second_normed = (hidden_state - second_mean) * second_scale
    second_inner = second_normed * second_gain + second_shift
    second_active = jax.nn.gelu(second_inner).astype(jnp.bfloat16)
    branch = (
        jnp.einsum("wbh,ch->wbc", second_active, point_full, preferred_element_type=jnp.float32)
        + point_bias
    )
    block = (source + branch).astype(jnp.bfloat16)
    window_part = block
    logits = jnp.einsum(
        "wbc,ct->wtb",
        window_part,
        lax.all_gather(head_weight, ("wide", "narrow"), axis=0, tiled=True),
        preferred_element_type=jnp.float32,
    )
    logits = logits + head_bias[None, :, None]
    tracks = jax.nn.softplus(logits).astype(jnp.bfloat16)
    grad_logits = (cot_tracks.astype(jnp.float32) * row_weight * jax.nn.sigmoid(logits)).astype(
        jnp.bfloat16
    )
    grad_block = jnp.einsum(
        "wtb,ct->wbc",
        grad_logits,
        lax.all_gather(head_weight, ("wide", "narrow"), axis=0, tiled=True),
        preferred_element_type=jnp.float32,
    )
    window_part = block
    grad_head = lax.psum_scatter(
        jnp.einsum("wbc,wtb->ct", window_part, grad_logits, preferred_element_type=jnp.float32),
        ("wide", "narrow"),
        scatter_dimension=0,
        tiled=True,
    )
    grad_summed = cot_block.astype(jnp.float32) * weight + grad_block
    grad_branch = grad_summed.astype(jnp.bfloat16)
    conv_full, point_full = (
        lax.all_gather(conv_weight, ("wide", "narrow"), axis=0, tiled=True),
        lax.all_gather(point_weight, ("wide", "narrow"), axis=0, tiled=True),
    )
    convolution_kernel = conv_full.reshape(3, -1, conv_full.shape[1])
    first_normed = (source - first_mean) * first_scale
    first_inner = first_normed * first_gain + first_shift
    hidden_state = convolve(padded_input, convolution_kernel, local_bin_count)
    second_normed = (hidden_state - second_mean) * second_scale
    second_inner = second_normed * second_gain + second_shift
    second_active = jax.nn.gelu(second_inner).astype(jnp.bfloat16)
    grad_point_local = jnp.einsum(
        "wbc,wbh->ch", grad_branch, second_active, preferred_element_type=jnp.float32
    )
    grad_second_active = jnp.einsum(
        "ldo,ov->ldv", grad_branch, point_full, preferred_element_type=jnp.float32
    )
    grad_second_inner = gelu_back(second_inner, grad_second_active)
    bias_point_local = jnp.sum(grad_branch.astype(jnp.float32), axis=(0, 1))
    bias_head_local = jnp.sum(grad_logits.astype(jnp.float32), axis=(0, 2))
    grad_second_gain, grad_second_shift, grad_point_bias, grad_head_bias = lax.psum(
        (
            jnp.sum(grad_second_inner * second_normed, axis=(0, 1)),
            jnp.sum(grad_second_inner, axis=(0, 1)),
            bias_point_local,
            bias_head_local,
        ),
        ("wide", "narrow"),
    )
    hidden_gradient = norm_back(
        grad_second_inner,
        second_normed,
        second_scale,
        second_gain,
        grad_second_gain,
        grad_second_shift,
        weight,
        counted,
    ).astype(jnp.bfloat16)
    padded_gradient = with_halo(hidden_gradient, (("narrow", 1),), DILATION_STEP)
    grad_first_active = jnp.einsum(
        "wbh,ch->wbc",
        padded_gradient[:, 2 * DILATION_STEP : 2 * DILATION_STEP + local_bin_count],
        convolution_kernel[0],
        preferred_element_type=jnp.float32,
    )
    for kernel_position in range(1, 3):
        start_offset = (2 - kernel_position) * DILATION_STEP
        grad_first_active = grad_first_active + jnp.einsum(
            "wbh,ch->wbc",
            padded_gradient[:, start_offset : start_offset + local_bin_count],
            convolution_kernel[kernel_position],
            preferred_element_type=jnp.float32,
        )
    grad_taps = [
        jnp.einsum(
            "wbc,wbh->ch",
            padded_input[
                :,
                kernel_position * DILATION_STEP : kernel_position * DILATION_STEP + local_bin_count,
            ],
            hidden_gradient,
            preferred_element_type=jnp.float32,
        )
        for kernel_position in range(3)
    ]
    grad_conv_local = jnp.concatenate(grad_taps, axis=0)
    grad_first_inner = gelu_back(first_inner, grad_first_active)
    grad_first_gain, grad_first_shift = lax.psum(
        (
            jnp.sum(grad_first_inner * first_normed, axis=(0, 1)),
            jnp.sum(grad_first_inner, axis=(0, 1)),
        ),
        ("wide", "narrow"),
    )
    grad_tokens = grad_summed + norm_back(
        grad_first_inner,
        first_normed,
        first_scale,
        first_gain,
        grad_first_gain,
        grad_first_shift,
        weight,
        counted,
    )
    grad_conv, grad_point = (
        lax.psum_scatter(grad_conv_local, ("wide", "narrow"), scatter_dimension=0, tiled=True),
        lax.psum_scatter(grad_point_local, ("wide", "narrow"), scatter_dimension=0, tiled=True),
    )
    return (
        block,
        tracks,
        grad_tokens,
        grad_conv,
        grad_point,
        grad_head,
        grad_first_gain,
        grad_first_shift,
        grad_second_gain,
        grad_second_shift,
        grad_point_bias,
        grad_head_bias,
    )


def solution(mesh):
    placed = (
        P("wide", "narrow", None),
        P("wide", "narrow"),
        P(("wide", "narrow"), None),
        P(("wide", "narrow"), None),
        P(("wide", "narrow"), None),
        P(),
        P(),
        P(),
        P(),
        P(),
        P(),
        P("wide", "narrow", None),
        P("wide", None, "narrow"),
    )
    return jax.shard_map(
        shards,
        mesh=mesh,
        in_specs=placed,
        out_specs=(
            P("wide", "narrow", None),
            P("wide", None, "narrow"),
            P("wide", "narrow", None),
            P(("wide", "narrow"), None),
            P(("wide", "narrow"), None),
            P(("wide", "narrow"), None),
            P(),
            P(),
            P(),
            P(),
            P(),
            P(),
        ),
        check_vma=False,
    )
```

profile of v0, /device:TPU:0, one launch (start us, length us, event | category | flops | bytes accessed | tf_op | source)
XLA Modules:
  0.0 800.7 jit_solution(4075093609060179027)
XLA Ops:
  10.8 3.0 fusion.36
  13.7 42.3 %all-reduce.4 = (f32[768]{0:T(1024)S(1)}, f32[]{:T(128)}) all-reduce(f32[768]{0:T(1024)S(1)} %fusion.36, f32[]{:T(128)} %convert_reduce_fusion.2), channel_id=1, replica_groups=mesh['wide'=8,'narrow'=4] {'wide','narrow'}, use_global_device_ids=true, to_apply=%region_1.0 | all-reduce | flops 769 | bytes 6152 | tf_op jit(solution)/shard_map/psum | solution.py:26
  56.7 2.9 fusion.38
  59.6 40.8 %psum.82 = f32[768]{0:T(1024)S(1)} all-reduce(f32[768]{0:T(1024)S(1)} %fusion.38), channel_id=1, replica_groups=mesh['wide'=8,'narrow'=4] {'wide','narrow'}, use_global_device_ids=true, to_apply=%region_5.0 | all-reduce | flops 768 | bytes 6144 | tf_op jit(solution)/shard_map/psum | solution.py:31
  101.1 5.4 fusion.24
  112.3 48.0 %all_gather.13 = bf16[768,384]{1,0:T(8,128)(2,1)S(1)} all-gather(bf16[24,384]{1,0:T(8,128)(2,1)S(1)} %copy-done.20), channel_id=1, replica_groups=mesh['wide'=8,'narrow'=4] {'wide','narrow'}, dimensions={0}, use_global_device_ids=true | all-gather | bytes 608256 | tf_op jit(solution)/shard_map/all_gather | solution.py:88
  160.3 4.7 fusion.60
  165.0 2.2 fusion.47
  167.3 4.1 multiply_reduce_fusion.1
  171.4 37.1 %psum.83 = f32[384]{0:T(512)S(1)} all-reduce(f32[384]{0:T(512)S(1)} %get-tuple-element.33), channel_id=1, replica_groups=mesh['wide'=8,'narrow'=4] {'wide','narrow'}, use_global_device_ids=true, to_apply=%region_7.0 | all-reduce | flops 384 | bytes 3072 | tf_op jit(solution)/shard_map/psum | solution.py:26
  209.2 2.7 fusion.46
  211.8 41.1 %psum.84 = f32[384]{0:T(512)S(1)} all-reduce(f32[384]{0:T(512)S(1)} %fusion.46), channel_id=1, replica_groups=mesh['wide'=8,'narrow'=4] {'wide','narrow'}, use_global_device_ids=true, to_apply=%region_9.0 | all-reduce | flops 384 | bytes 3072 | tf_op jit(solution)/shard_map/psum | solution.py:31
  253.7 8.8 %fusion.37 = bf16[10,256,768]{2,1,0:T(8,128)(2,1)} fusion(bf16[10,256,768]{2,1,0:T(8,128)(2,1)} %param.13, f32[768]{0:T(1024)S(1)} %copy-done.34, bf16[768,384]{1,0:T(8,128)(2,1)S(1)} %all_gather.13, f32[10,256,384]{2,1,0:T(8,128)} %get-tuple-element.34, f32[384]{0:T(512)S(1)} %copy-done.35, f32[384]{0:T(512)S(1)} %copy-done.21, ...), kind=kOutput, calls=%fused_computation.49 | convolution fusion | flops 1530593280 | bytes 12395520 | tf_op jit(solution)/shard_map/wbh,ch->wbc/dot_general | solution.py:102
  262.5 73.0 %convert_reduce_fusion = (f32[5313]{0:T(1024)S(1)}, bf16[10,5313,256]{2,1,0:T(8,128)(2,1)}, bf16[10,5313,256]{2,1,0:T(8,128)(2,1)}) fusion(f32[5313]{0:T(1024)S(1)} %copy-done.33, f32[10,256]{1,0:T(8,128)S(1)} %convert_element_type.42, bf16[10,5313,256]{2,1,0:T(8,128)(2,1)} %param.25, bf16[10,256,768]{2,1,0:T(8,128)(2,1)} %fusion.37, ...), kind=kOutput, calls=%fused_computation.13 | convolution fusion | flops 21122775040 | bytes 93753352 | tf_op jit(solution)/shard_map/wbc,ct->wtb/dot_general | solution.py:107
  335.6 41.4 %convert_reduce_fusion.1 = (f32[768]{0:T(1024)S(1)}, bf16[10,256,768]{2,1,0:T(8,128)(2,1)S(1)}, f32[10,256,768]{2,1,0:T(8,128)}) fusion(f32[10,256]{1,0:T(8,128)S(1)} %convert_element_type.42, bf16[10,256,768]{2,1,0:T(8,128)(2,1)} %param.24, bf16[10,5313,256]{2,1,0:T(8,128)(2,1)} %get-tuple-element.25, bf16[768,5313]{1,0:T(8,128)(2,1)} %all-gather.5.cloned.1.call-done), kind=kOutput, calls=%fused_computation.51 | convolution fusion | flops 20903362560 | bytes 51105280 | tf_op jit(solution)/shard_map/wtb,ct->wbc/dot_general | solution.py:118
  379.0 3.4 convolution_bitcast_fusion.1
  382.4 8.9 %fusion.68 = (f32[384]{0:T(512)S(1)}, f32[384]{0:T(512)S(1)}, f32[10,256,384]{2,1,0:T(8,128)}) fusion(f32[384]{0:T(512)S(1)} %copy-done.24, f32[10,256,384]{2,1,0:T(8,128)} %get-tuple-element.34, f32[384]{0:T(512)S(1)} %copy-done.19, f32[384]{0:T(512)S(1)} %copy-done.36, f32[384]{0:T(512)S(1)} %copy-done.22, bf16[10,256,768]{2,1,0:T(8,128)(2,1)} %copy-done.37, ...), kind=kOutput, calls=%fused_computation.108 | convolution fusion | flops 1535507712 | bytes 12395520 | tf_op jit(solution)/shard_map/ldo,ov->ldv/dot_general | solution.py:147
  391.3 39.6 %all-reduce.3 = (f32[384]{0:T(512)S(1)}, f32[384]{0:T(512)S(1)}) all-reduce(f32[384]{0:T(512)S(1)} %get-tuple-element.15, f32[384]{0:T(512)S(1)} %get-tuple-element.14), channel_id=1, replica_groups=mesh['wide'=8,'narrow'=4] {'wide','narrow'}, use_global_device_ids=true, to_apply=%region_13.14 | all-reduce | flops 768 | bytes 6144 | tf_op jit(solution)/shard_map/psum | solution.py:153
  430.9 4.1 multiply_convert_fusion
  435.4 2.2 fusion.55
  437.6 2.3 fusion.56
  439.9 2.2 convolution_bitcast_fusion.2
  442.1 2.1 pad_maximum_fusion.2
  444.3 29.4 %convolution_bitcast_fusion = f32[768,5313]{1,0:T(8,128)} fusion(bf16[10,256,768]{2,1,0:T(8,128)(2,1)} %fusion.37, bf16[10,5313,256]{2,1,0:T(8,128)(2,1)} %get-tuple-element.25), kind=kOutput, calls=%fused_computation.19 | convolution fusion | flops 20891566080 | bytes 47456256 | tf_op jit(solution)/shard_map/wbc,wtb->ct/dot_general | solution.py:126
  475.1 3.0 collective-permute-start.3
  478.1 3.3 fusion.59
  481.5 3.5 fusion.53
  485.0 11.6 %fusion.67 = (f32[768]{0:T(1024)S(1)}, f32[768]{0:T(1024)S(1)}, f32[10,256,768]{2,1,0:T(8,128)}) fusion(f32[768]{0:T(1024)S(1)} %copy-done.17, f32[768]{0:T(1024)S(1)} %copy-done.13, bf16[10,256,768]{2,1,0:T(8,128)(2,1)S(1)} %copy-done, f32[768]{0:T(1024)S(1)} %copy-done.26, f32[768]{0:T(1024)S(1)} %copy-done.15, ...), kind=kOutput, calls=%fused_computation.107 | convolution fusion | flops 1570896384 | bytes 30183936 | tf_op jit(solution)/shard_map/wbh,ch->wbc/dot_general | solution.py:181
  496.6 41.1 %all-reduce.2 = (f32[768]{0:T(1024)S(1)}, f32[768]{0:T(1024)S(1)}, f32[768]{0:T(1024)}, f32[5313]{0:T(1024)}) all-reduce(f32[768]{0:T(1024)S(1)} %get-tuple-element.13, f32[768]{0:T(1024)S(1)} %get-tuple-element.12, f32[768]{0:T(1024)S(1)} %get-tuple-element.26, ...), channel_id=1, replica_groups=mesh['wide'=8,'narrow'=4] {'wide','narrow'}, use_global_device_ids=true, to_apply=%region_17.18 | all-reduce | flops 7617 | bytes 60936 | tf_op jit(solution)/shard_map/psum | solution.py:201
  537.7 13.5 %fusion.31 = f32[10,256,768]{2,1,0:T(8,128)} fusion(bf16[10,256,768]{2,1,0:T(8,128)(2,1)} %param.13, f32[10,256,768]{2,1,0:T(8,128)} %get-tuple-element.37, f32[10,256,768]{2,1,0:T(8,128)} %get-tuple-element.35, bf16[10,256,768]{2,1,0:T(8,128)(2,1)} %param.24, f32[768]{0:T(1024)S(1)} %get-tuple-element.16, f32[768]{0:T(1024)S(1)} %mul.333, ...), kind=kLoop, calls=%fused_computation.43 | loop fusion | flops 27525120 | bytes 31493120 | tf_op jit(solution)/shard_map/add | solution.py:208
  551.3 45.8 %reduce-scatter.10.cloned.1.call-done = f32[72,384]{1,0:T(8,128)} async-done(((f32[2304,384]{1,0:T(8,128)}), f32[72,384]{1,0:T(8,128)}) %reduce-scatter.10.cloned.1.call-update) | async-done | bytes 110608
  597.0 196.7 %reduce-scatter.8.cloned.1.call-done = f32[24,5313]{1,0:T(8,128)} async-done(((f32[768,5313]{1,0:T(8,128)}), f32[24,5313]{1,0:T(8,128)}) %reduce-scatter.8.cloned.1.call-update) | async-done | bytes 510064 | tf_op jit(solution)/shard_map/reduce_scatter | solution.py:125
  (107 shorter events, 15.8 us)
Async XLA Ops:
  7.2 153.1 %all-gather.3.cloned.1.call-start = ((), (), s32[]{:S(2)}) async-start(), calls=%async_computation.3 | async-start | bytes 1824768 | tf_op jit(solution)/shard_map/all_gather | solution.py:87
  7.9 254.6 %all-gather.5.cloned.1.call-start = ((), (), s32[]{:S(2)}) async-start(), calls=%async_computation.4 | async-start | bytes 8515584 | tf_op jit(solution)/shard_map/all_gather | solution.py:110
  8.7 542.6 %reduce-scatter.12.cloned.1.call-start = ((), (), s32[]{:S(2)}) async-start(), calls=%async_computation.7 | async-start | bytes 1216512
  10.8 90.3 %copy-start.14 = (f32[768]{0:T(1024)S(1)}, f32[768]{0:T(1024)}, u32[]{:S(2)}) copy-start(f32[768]{0:T(1024)} %param.18) | copy-start | bytes 9220
  10.8 90.3 %copy-start.25 = (f32[768]{0:T(1024)S(1)}, f32[768]{0:T(1024)}, u32[]{:S(2)}) copy-start(f32[768]{0:T(1024)} %param.19) | copy-start | bytes 9220
  56.7 49.8 %copy-start.12 = (f32[768]{0:T(1024)}, f32[768]{0:T(1024)S(1)}, u32[]{:S(2)}) copy-start(f32[768]{0:T(1024)S(1)} %broadcast_divide_fusion.1) | copy-start | bytes 9220
  101.0 5.4 copy-start.16
  101.1 10.0 %copy-start.11 = (s32[10,256]{1,0:T(8,128)S(1)}, s32[10,256]{1,0:T(8,128)}, u32[]{:S(2)}) copy-start(s32[10,256]{1,0:T(8,128)} %param.14) | copy-start | bytes 30724
  101.1 11.2 %copy-start.20 = (bf16[24,384]{1,0:T(8,128)(2,1)S(1)}, bf16[24,384]{1,0:T(8,128)(2,1)}, u32[]{:S(2)}) copy-start(bf16[24,384]{1,0:T(8,128)(2,1)} %param.16) | copy-start | bytes 55300
  108.4 56.6 %collective-permute-start = (bf16[10,11,768]{2,1,0:T(8,128)(2,1)S(1)}, bf16[10,11,768]{2,1,0:T(8,128)(2,1)S(1)}, u32[]{:S(2)}, u32[]{:S(2)}) collective-permute-start(bf16[10,11,768]{2,1,0:T(8,128)(2,1)S(1)} %get-tuple-element.30), channel_id=1, source_target_pairs={{0,1},{1,2},{2,3},{4,5},{5,6},{6,7},{8,9},{9,10},{10,11},{12,13},{... | collective-permute-start | bytes 506888 | tf_op jit(solution)/shard_map/ppermute | solution.py:19
  109.7 57.5 %collective-permute-start.1 = (bf16[10,11,768]{2,1,0:T(8,128)(2,1)S(1)}, bf16[10,11,768]{2,1,0:T(8,128)(2,1)S(1)}, u32[]{:S(2)}, u32[]{:S(2)}) collective-permute-start(bf16[10,11,768]{2,1,0:T(8,128)(2,1)S(1)} %get-tuple-element.29), channel_id=1, source_target_pairs={{1,0},{2,1},{3,2},{5,4},{6,5},{7,6},{9,8},{10,9},{11,10},{13,12},{... | collective-permute-start | bytes 506888 | tf_op jit(solution)/shard_map/ppermute | solution.py:20
  160.3 93.4 %copy-start.6 = (bf16[768,384]{1,0:T(8,128)(2,1)}, bf16[768,384]{1,0:T(8,128)(2,1)S(1)}, u32[]{:S(2)}) copy-start(bf16[768,384]{1,0:T(8,128)(2,1)S(1)} %all_gather.13) | copy-start | bytes 1769476
  160.3 4.7 copy-start.2
  160.3 4.7 copy-start.5
  171.4 82.3 %copy-start.21 = (f32[384]{0:T(512)S(1)}, f32[384]{0:T(512)}, u32[]{:S(2)}) copy-start(f32[384]{0:T(512)} %param.20) | copy-start | bytes 4612
  171.4 82.3 %copy-start.34 = (f32[768]{0:T(1024)S(1)}, f32[768]{0:T(1024)}, u32[]{:S(2)}) copy-start(f32[768]{0:T(1024)} %param.22) | copy-start | bytes 9220
  171.4 82.3 %copy-start.35 = (f32[384]{0:T(512)S(1)}, f32[384]{0:T(512)}, u32[]{:S(2)}) copy-start(f32[384]{0:T(512)} %param.21) | copy-start | bytes 4612
  209.2 53.4 %copy-start.18 = (f32[384]{0:T(512)}, f32[384]{0:T(512)S(1)}, u32[]{:S(2)}) copy-start(f32[384]{0:T(512)S(1)} %broadcast_divide_fusion.2) | copy-start | bytes 4612
  253.7 8.8 %copy-start.23 = (f32[384]{0:T(512)}, f32[384]{0:T(512)S(1)}, u32[]{:S(2)}) copy-start(f32[384]{0:T(512)S(1)} %add_rsqrt_fusion.1) | copy-start | bytes 4612
  253.7 8.8 %copy-start.33 = (f32[5313]{0:T(1024)S(1)}, f32[5313]{0:T(1024)}, u32[]{:S(2)}) copy-start(f32[5313]{0:T(1024)} %param.23) | copy-start | bytes 63760
  335.5 43.4 %copy-start.4 = (f32[10,256,384]{2,1,0:T(8,128)S(1)}, f32[10,256,384]{2,1,0:T(8,128)}, u32[]{:S(2)}) copy-start(f32[10,256,384]{2,1,0:T(8,128)} %get-tuple-element.34) | copy-start | bytes 11796484
  335.6 43.4 %copy-start.19 = (f32[384]{0:T(512)S(1)}, f32[384]{0:T(512)}, u32[]{:S(2)}) copy-start(f32[384]{0:T(512)} %copy-done.18) | copy-start | bytes 4612
  335.6 43.4 %copy-start.22 = (f32[384]{0:T(512)S(1)}, f32[384]{0:T(512)}, u32[]{:S(2)}) copy-start(f32[384]{0:T(512)} %param.20) | copy-start | bytes 4612
  335.6 43.4 %copy-start.24 = (f32[384]{0:T(512)S(1)}, f32[384]{0:T(512)}, u32[]{:S(2)}) copy-start(f32[384]{0:T(512)} %copy-done.23) | copy-start | bytes 4612
  335.6 43.4 %copy-start.36 = (f32[384]{0:T(512)S(1)}, f32[384]{0:T(512)}, u32[]{:S(2)}) copy-start(f32[384]{0:T(512)} %param.21) | copy-start | bytes 4612
  382.4 48.5 %copy-start.10 = (f32[10,256]{1,0:T(8,128)S(1)}, f32[10,256]{1,0:T(8,128)}, u32[]{:S(2)}) copy-start(f32[10,256]{1,0:T(8,128)} %broadcast_divide_fusion) | copy-start | bytes 30724
  391.3 205.8 %reduce-scatter.10.cloned.1.call-start = ((), (), s32[]{:S(2)}) async-start(), calls=%async_computation.6 | async-start | bytes 3649536
  444.2 349.5 %reduce-scatter.8.cloned.1.call-start = ((), (), s32[]{:S(2)}) async-start(), calls=%async_computation.5 | async-start | bytes 17031168 | tf_op jit(solution)/shard_map/reduce_scatter | solution.py:125
  473.8 7.7 collective-permute-start.2
  475.1 9.9 %collective-permute-start.3 = (bf16[10,11,384]{2,1,0:T(8,128)(2,1)S(1)}, bf16[10,11,384]{2,1,0:T(8,128)(2,1)S(1)}, u32[]{:S(2)}, u32[]{:S(2)}) collective-permute-start(bf16[10,11,384]{2,1,0:T(8,128)(2,1)S(1)} %get-tuple-element.31), channel_id=1, source_target_pairs={{0,1},{1,2},{2,3},{4,5},{5,6},{6,7},{8,9},{9,10},{10,11},{12,13},{... | collective-permute-start | bytes 253448 | tf_op jit(solution)/shard_map/ppermute | solution.py:19
  537.7 13.5 %copy-start.27 = (f32[768]{0:T(1024)}, f32[768]{0:T(1024)S(1)}, u32[]{:S(2)}) copy-start(f32[768]{0:T(1024)S(1)} %get-tuple-element.16) | copy-start | bytes 9220
  537.7 13.5 %copy-start.28 = (f32[768]{0:T(1024)}, f32[768]{0:T(1024)S(1)}, u32[]{:S(2)}) copy-start(f32[768]{0:T(1024)S(1)} %get-tuple-element.17) | copy-start | bytes 9220
  (15 other events, 50.8 us)
Sparse Core Ops, SparseCore 0:
  10.8 58.2 all-gather.2
  72.0 79.8 all-gather.4
  391.4 97.2 reduce-scatter.11
  494.6 102.4 reduce-scatter.9
  603.8 189.8 reduce-scatter.7
where the time goes:
time: 810 us; the launch traced here: 801 us
  blocking collectives  290 us (36%)
  waiting for transfers between devices  244 us (30%)
  matrix products  201 us (25%)
  other arithmetic  39.6 us (5%)
  between operations  14.8 us (2%)
    reduce_scatter x1, waiting for transfers between devices, shards(): lax.psum_scatter(jnp.einsum('wbc,wtb->ct', window_part, grad_logits, pref...  197 us
    psum x2, blocking collectives, norm_stats(): lax.psum(jnp.sum(weight * centred * centred, axis=(0, 1)), ('wide', 'narr...  81.9 us
    psum x2, blocking collectives, norm_stats(): lax.psum((jnp.sum(values * weight, axis=(0, 1)), jnp.sum(weight)), ('wide...  79.4 us
    dot_general x1, matrix products, shards(): jnp.einsum('wbc,ct->wtb', window_part, lax.all_gather(head_weight, ('wide...  73 us
    all_gather x1, blocking collectives, shards(): lax.all_gather(point_weight, ('wide', 'narrow'), axis=0, tiled=True)  48 us
    unnamed x7, waiting for transfers between devices  47.2 us
    dot_general x1, matrix products, shards(): jnp.einsum('wtb,ct->wbc', grad_logits, lax.all_gather(head_weight, ('wide...  41.4 us
    psum x1, blocking collectives, shards(): lax.psum((jnp.sum(grad_first_inner * first_normed, axis=(0, 1)), jnp.sum(...  41.1 us
  transfers between devices with their start and end apart: 9, of which 2 were waited for; matrix products, arithmetic and copies ran while one was open for 14% of the time, Pallas kernels for 0%

commit v1 on v0

v1 whole, which is shorter than its diff:
```python
import jax
import jax.numpy as jnp
from jax import lax
from jax.sharding import PartitionSpec as P

DILATION_STEP = 11
BOTH = ("wide", "narrow")
F32 = jnp.float32
BF16 = jnp.bfloat16


epsilon = 1e-05


def axis_bits():
    found = []
    for axis in ("narrow", "wide"):
        count = lax.axis_size(axis)
        assert count & (count - 1) == 0
        found += [(axis, count, bit) for bit in range(count.bit_length() - 1)]
    return found


def swap(value, axis, count, bit):
    return lax.ppermute(value, axis, [(i, i ^ (1 << bit)) for i in range(count)])


def my_bit(axis, bit):
    return (lax.axis_index(axis) >> bit) & 1


def sum_all(value):
    for axis, count, bit in axis_bits():
        value = value + swap(value, axis, count, bit)
    return value


def gather_rows(shard):
    rows, columns = shard.shape
    held = shard[None]
    for axis, count, bit in reversed(axis_bits()):
        other = swap(held, axis, count, bit)
        low = my_bit(axis, bit) == 0
        first = jnp.where(low, held, other)
        second = jnp.where(low, other, held)
        held = jnp.stack([first, second], axis=1).reshape(-1, rows, columns)
    return held


def scatter_rows(value):
    rows, columns = value.shape[1:]
    for axis, count, bit in axis_bits():
        pairs = value.reshape(-1, 2, rows, columns)
        mine = my_bit(axis, bit)
        send = lax.dynamic_index_in_dim(pairs, 1 - mine, axis=1, keepdims=False)
        keep = lax.dynamic_index_in_dim(pairs, mine, axis=1, keepdims=False)
        got = swap(send, axis, count, bit)
        value = (keep.astype(F32) + got.astype(F32)).astype(value.dtype)
    return value[0]


def halos(first, last, axis):
    count = lax.axis_size(axis)
    up = [(i, i + 1) for i in range(count - 1)]
    down = [(i + 1, i) for i in range(count - 1)]
    return lax.ppermute(last, axis, up), lax.ppermute(first, axis, down)


def edges(value):
    return value[:, :DILATION_STEP], value[:, value.shape[1] - DILATION_STEP :]


def norm_stats(values, weight):
    channels = values.shape[-1]
    number = jnp.sum(weight)
    total = jnp.sum(values * weight, axis=(0, 1))
    centred = values - total / jnp.maximum(number, 1.0)
    spread = jnp.sum(weight * centred * centred, axis=(0, 1))
    packed = jnp.stack([total, spread, jnp.broadcast_to(number, (channels,))])
    for axis, count, bit in axis_bits():
        other = swap(packed, axis, count, bit)
        n_a, n_b = packed[2], other[2]
        both = n_a + n_b
        gap = packed[0] / jnp.maximum(n_a, 1.0) - other[0] / jnp.maximum(n_b, 1.0)
        merged = packed[1] + other[1] + gap * gap * (n_a * n_b / jnp.maximum(both, 1.0))
        packed = jnp.stack([packed[0] + other[0], merged, both])
    counted = packed[2]
    return packed[0] / counted, lax.rsqrt(packed[1] / counted + epsilon), counted


def gelu_back(preact, upstream):
    return jax.vjp(jax.nn.gelu, preact)[1](upstream)[0]


def norm_back(grad_inner, normed, scale_inv, gain, grad_gain, grad_shift, weight, counted):
    grad_normed = grad_inner * gain
    return scale_inv * (
        grad_normed - weight / counted * (gain * grad_shift + normed * gain * grad_gain)
    )


def shards(
    tokens,
    usable,
    conv_weight,
    point_weight,
    head_weight,
    first_gain,
    first_shift,
    second_gain,
    second_shift,
    point_bias,
    head_bias,
    cot_block,
    cot_tracks,
):
    windows, bins, channels = tokens.shape
    filters = conv_weight.shape[1]
    devices = lax.axis_size("wide") * lax.axis_size("narrow")
    own = channels // devices
    weight = usable.astype(F32)[:, :, None]
    row_weight = usable.astype(F32)[:, None, :]
    source = tokens.astype(F32)
    head_full = lax.all_gather(head_weight, BOTH, axis=0, tiled=True)
    small = gather_rows(
        jnp.concatenate([conv_weight.reshape(own, 3 * filters), point_weight], axis=1)
    )
    kernel = small[:, :, : 3 * filters].reshape(3, channels, filters)
    point_full = small[:, :, 3 * filters :].reshape(channels, filters)

    before, after = halos(*edges(tokens), "narrow")
    padded = jnp.concatenate([before, tokens, after], axis=1).astype(F32)
    place = lax.axis_index("narrow") * bins + jnp.arange(-DILATION_STEP, bins + DILATION_STEP)
    inside = (place >= 0) & (place < bins * lax.axis_size("narrow"))
    inside = inside[None, :, None]

    first_mean, first_scale, counted = norm_stats(source, weight)
    padded_inner = (padded - first_mean) * first_scale * first_gain + first_shift
    padded_input = jnp.where(inside, jax.nn.gelu(padded_inner), 0.0).astype(BF16)
    taps = [padded_input[:, k * DILATION_STEP : k * DILATION_STEP + bins] for k in range(3)]
    hidden = sum(
        jnp.einsum("ldo,ov->ldv", taps[k], kernel[k], preferred_element_type=F32) for k in range(3)
    )
    second_mean, second_scale, counted_two = norm_stats(hidden, weight)
    second_normed = (hidden - second_mean) * second_scale
    second_inner = second_normed * second_gain + second_shift
    second_active = jax.nn.gelu(second_inner).astype(BF16)
    branch = (
        jnp.einsum("wbh,ch->wbc", second_active, point_full, preferred_element_type=F32)
        + point_bias
    )
    block = (source + branch).astype(BF16)

    logits = jnp.einsum("wbc,ct->wtb", block, head_full, preferred_element_type=F32)
    logits = logits + head_bias[None, :, None]
    tracks = jax.nn.softplus(logits).astype(BF16)
    grad_logits = (cot_tracks.astype(F32) * row_weight * jax.nn.sigmoid(logits)).astype(BF16)
    grad_head_local = jnp.einsum(
        "wbc,wtb->ct", block, grad_logits, preferred_element_type=F32
    ).astype(BF16)
    grad_head = scatter_rows(grad_head_local.reshape(devices, own, -1)).astype(F32)
    grad_block = jnp.einsum("wtb,ct->wbc", grad_logits, head_full, preferred_element_type=F32)
    grad_summed = cot_block.astype(F32) * weight + grad_block
    grad_branch = grad_summed.astype(BF16)
    grad_point_local = jnp.einsum(
        "wbc,wbh->ch", grad_branch, second_active, preferred_element_type=F32
    )
    grad_second_active = jnp.einsum(
        "wbc,ch->wbh", grad_branch, point_full, preferred_element_type=F32
    )
    grad_second_inner = gelu_back(second_inner, grad_second_active)
    before, after = halos(
        *edges(jnp.concatenate([grad_second_inner, second_normed], axis=2)), "narrow"
    )
    weight_before, weight_after = halos(*edges(weight[:, :, 0]), "narrow")
    sums = sum_all(
        jnp.concatenate(
            [
                jnp.sum(grad_second_inner * second_normed, axis=(0, 1)),
                jnp.sum(grad_second_inner, axis=(0, 1)),
                jnp.sum(grad_branch.astype(F32), axis=(0, 1)),
                jnp.sum(grad_logits.astype(F32), axis=(0, 2)),
            ]
        )
    )
    grad_second_gain = sums[:filters]
    grad_second_shift = sums[filters : 2 * filters]
    grad_point_bias = sums[2 * filters : 2 * filters + channels]
    grad_head_bias = sums[2 * filters + channels :]

    def hidden_back(inner, normed, row):
        return norm_back(
            inner,
            normed,
            second_scale,
            second_gain,
            grad_second_gain,
            grad_second_shift,
            row,
            counted[0],
        ).astype(BF16)

    hidden_gradient = hidden_back(grad_second_inner, second_normed, weight)
    padded_gradient = jnp.concatenate(
        [
            hidden_back(before[..., :filters], before[..., filters:], weight_before[:, :, None]),
            hidden_gradient,
            hidden_back(after[..., :filters], after[..., filters:], weight_after[:, :, None]),
        ],
        axis=1,
    )
    grad_taps = [
        jnp.einsum("wbc,wbh->ch", taps[k], hidden_gradient, preferred_element_type=F32)
        for k in range(3)
    ]
    grad_small = jnp.concatenate(
        [
            jnp.concatenate(grad_taps, axis=0).astype(BF16).reshape(devices, own, 3 * filters),
            grad_point_local.astype(BF16).reshape(devices, own, filters),
        ],
        axis=2,
    )
    grad_small = scatter_rows(grad_small).astype(F32)
    grad_conv = grad_small[:, : 3 * filters].reshape(3 * own, filters)
    grad_point = grad_small[:, 3 * filters :]

    grad_first_active = sum(
        jnp.einsum(
            "wbh,ch->wbc",
            padded_gradient[:, (2 - k) * DILATION_STEP : (2 - k) * DILATION_STEP + bins],
            kernel[k],
            preferred_element_type=F32,
        )
        for k in range(3)
    )
    first_normed = (source - first_mean) * first_scale
    first_inner = first_normed * first_gain + first_shift
    grad_first_inner = gelu_back(first_inner, grad_first_active)
    sums = sum_all(
        jnp.stack(
            [
                jnp.sum(grad_first_inner * first_normed, axis=(0, 1)),
                jnp.sum(grad_first_inner, axis=(0, 1)),
            ]
        )
    )
    grad_first_gain, grad_first_shift = sums[0], sums[1]
    grad_tokens = grad_summed + norm_back(
        grad_first_inner,
        first_normed,
        first_scale,
        first_gain,
        grad_first_gain,
        grad_first_shift,
        weight,
        counted,
    )
    return (
        block,
        tracks,
        grad_tokens,
        grad_conv,
        grad_point,
        grad_head,
        grad_first_gain,
        grad_first_shift,
        grad_second_gain,
        grad_second_shift,
        grad_point_bias,
        grad_head_bias,
    )


def solution(mesh):
    rows = P("wide", "narrow", None)
    split = P(("wide", "narrow"), None)
    tracks = P("wide", None, "narrow")
    return jax.shard_map(
        shards,
        mesh=mesh,
        in_specs=(
            (rows, P("wide", "narrow"), split, split, split) + (P(),) * 6 + (rows, tracks)
        ),
        out_specs=(rows, tracks, rows, split, split, split) + (P(),) * 6,
        check_vma=False,
    )
```

time: 810 us -> 482 us (0.60)
  blocking collectives: 290 us -> 0 us
  waiting for transfers between devices: 244 us -> 130 us
  starting transfers between devices: 7.12 us -> 52.1 us
  local copies, waits for them, and re-layouts: 4.39 us -> 39 us
  matrix products: 201 us -> 185 us
  other arithmetic: 39.6 us -> 55.6 us
    psum x6 -> x0, blocking collectives: 242 us -> none  [the longest x2 81.9 us: norm_stats(): lax.psum(jnp.sum(weight * centred * centred, axis=(0, 1)), ('wide', 'narr...]
    reduce_scatter x1 -> x0, waiting for transfers between devices: 197 us -> none  [shards(): lax.psum_scatter(jnp.einsum('wbc,wtb->ct', window_part, grad_logits, pref...]
    ppermute x4 -> x41, waiting for transfers between devices: 0.01 us -> 129 us  [the longest x35 129 us: swap(): return lax.ppermute(value, axis, [(i, i ^ 1 << bit) for i in range(count)])]
    all_gather x1 -> x0, blocking collectives: 48 us -> none  [shards(): lax.all_gather(point_weight, ('wide', 'narrow'), axis=0, tiled=True)]
    unnamed x7 -> x1, waiting for transfers between devices: 47.2 us -> 0.68 us
    ppermute x4 -> x41, starting transfers between devices: 6.93 us -> 52.1 us  [the longest x35 39.7 us: swap(): return lax.ppermute(value, axis, [(i, i ^ 1 << bit) for i in range(count)])]
    convert_element_type x0 -> x2, local copies, waits for them, and re-layouts: none -> 15.1 us  [the longest x1 11.2 us: shards(): grad_head_local = jnp.einsum('wbc,wtb->ct', block, grad_logits, preferred...]
    convert_element_type x3 -> x14, other arithmetic: 10.2 us -> 23.5 us  [the longest x1 9.73 us: shards(): jnp.where(inside, jax.nn.gelu(padded_inner), 0.0).astype(BF16)]
  transfers between devices with their start and end apart: 9 -> 42, of which waited for: 2 -> 17; matrix products, arithmetic and copies ran while one was open for 14% -> 57% of each run, Pallas kernels for 0% -> 0%
where the time goes in v1:
time: 482 us; the launch traced here: 478 us
  matrix products  185 us (38%)
  waiting for transfers between devices  130 us (27%)
  other arithmetic  55.6 us (12%)
  starting transfers between devices  52.1 us (11%)
  local copies, waits for them, and re-layouts  39 us (8%)
  between operations  16.4 us (3%)
    ppermute x35, waiting for transfers between devices, swap(): return lax.ppermute(value, axis, [(i, i ^ 1 << bit) for i in range(count)])  129 us
    dot_general x1, matrix products, shards(): jnp.einsum('wbc,ct->wtb', block, head_full, preferred_element_type=F32)  73 us
    ppermute x35, starting transfers between devices, swap(): return lax.ppermute(value, axis, [(i, i ^ 1 << bit) for i in range(count)])  39.7 us
    dot_general x1, matrix products, shards(): jnp.einsum('wtb,ct->wbc', grad_logits, head_full, preferred_element_type=...  30.1 us
    dot_general x1, matrix products, shards(): jnp.einsum('wbc,wtb->ct', block, grad_logits, preferred_element_type=F32)  27.7 us
    dot_general x3, matrix products, shards(): jnp.einsum('wbh,ch->wbc', padded_gradient[:, (2 - k) * DILATION_STEP:(2 -...  19.9 us
    ppermute x6, starting transfers between devices, halos(): return (lax.ppermute(last, axis, up), lax.ppermute(first, axis, down))  12.4 us
    dot_general x3, matrix products, shards(): jnp.einsum('ldo,ov->ldv', taps[k], kernel[k], preferred_element_type=F32)  11.8 us
  transfers between devices with their start and end apart: 42, of which 17 were waited for; matrix products, arithmetic and copies ran while one was open for 57% of the time, Pallas kernels for 0%

profile of v1, /device:TPU:0, one launch (start us, length us, event | category | flops | bytes accessed | tf_op | source)
XLA Modules:
  0.0 477.5 jit_solution(17475584344689874612)
XLA Ops:
  8.6 3.0 fusion.34
  12.9 2.9 fusion.33
  25.8 5.3 %collective-permute-done.7 = bf16[1,24,1536]{2,1,0:T(8,128)(2,1)S(1)} collective-permute-done((bf16[1,24,1536]{2,1,0:T(8,128)(2,1)S(1)}, bf16[1,24,1536]{2,1,0:T(8,128)(2,1)S(1)}, u32[]{:S(2)}, u32[]{:S(2)}) %collective-permute-start.7) | collective-permute-done | bytes 73760 | tf_op jit(solution)/shard_map/ppermute | solution.py:25
  33.4 3.6 collective-permute-done.8
  42.7 4.6 collective-permute-done.9
  47.6 5.5 %collective-permute-start.6 = (f32[3,768]{1,0:T(4,128)S(1)}, f32[3,768]{1,0:T(4,128)S(1)}, u32[]{:S(2)}, u32[]{:S(2)}) collective-permute-start(f32[3,768]{1,0:T(4,128)S(1)} %pad_maximum_fusion.16), channel_id=1, source_target_pairs={{0,16},{4,20},{8,24},{12,28},{16,0},{20,4},{24,8},{28,12},{1,17},{... | collective-permute-start | bytes 27656 | tf_op jit(solution)/shard_map/ppermute | solution.py:25
  54.9 11.8 %collective-permute-done.10 = bf16[8,24,1536]{2,1,0:T(8,128)(2,1)S(1)} collective-permute-done((bf16[8,24,1536]{2,1,0:T(8,128)(2,1)S(1)}, bf16[8,24,1536]{2,1,0:T(8,128)(2,1)S(1)}, u32[]{:S(2)}, u32[]{:S(2)}) %collective-permute-start.10) | collective-permute-done | bytes 589856 | tf_op jit(solution)/shard_map/ppermute | solution.py:25
  67.2 9.7 %fusion.18 = bf16[10,278,768]{2,1,0:T(8,128)(2,1)} fusion(bf16[10,11,768]{2,1,0:T(8,128)(2,1)S(1)} %collective-permute-done.1, bf16[10,256,768]{2,1,0:T(8,128)(2,1)S(1)} %copy-done, bf16[10,11,768]{2,1,0:T(8,128)(2,1)S(1)} %collective-permute-done, f32[768]{0:T(1024)S(1)} %copy-done.38, f32[768]{0:T(1024)S(1)} %copy-done.24, f32[768]{0:T(1024)S(1)} %add_rsqrt_fusion, ...), kind=kLoop, calls=%fused_computation.32 | loop fusion | flops 42700800 | bytes 8552726 | tf_op jit(solution)/shard_map/convert_element_type | solution.py:139
  79.0 3.9 reshape.663
  82.9 4.8 %fusion.65 = f32[10,256,384]{2,1,0:T(8,128)S(1)} fusion(bf16[10,278,768]{2,1,0:T(8,128)(2,1)} %fusion.18, bf16[3,768,384]{2,1,0:T(8,128)(2,1)} %reshape.663), kind=kOutput, calls=%fused_computation.95 | convolution fusion | flops 1509949440 | bytes 8454144 | tf_op jit(solution)/shard_map/ldo,ov->ldv/dot_general | solution.py:142
  87.7 4.4 fusion.61
  100.0 3.6 collective-permute-done.13
  107.1 3.4 collective-permute-start.25
  124.3 4.8 fusion.35
  129.1 73.0 %convert_reduce_fusion = (f32[5313]{0:T(1024)S(1)}, bf16[10,5313,256]{2,1,0:T(8,128)(2,1)}, bf16[10,5313,256]{2,1,0:T(8,128)(2,1)}) fusion(f32[5313]{0:T(1024)S(1)} %copy-done.40, f32[10,256]{1,0:T(8,128)S(1)} %convert_element_type.193, bf16[10,5313,256]{2,1,0:T(8,128)(2,1)} %param.25, bf16[10,256,768]{2,1,0:T(8,128)(2,1)} %fusion.35, ...), kind=kOutput, calls=%fused_computation.13 | convolution fusion | flops 21122775040 | bytes 93753352 | tf_op jit(solution)/shard_map/wbc,ct->wtb/dot_general | solution.py:154
  202.1 30.1 %convert_reduce_fusion.1 = (f32[768]{0:T(1024)S(1)}, bf16[10,256,768]{2,1,0:T(8,128)(2,1)}, f32[10,256,768]{2,1,0:T(8,128)}) fusion(f32[10,256]{1,0:T(8,128)S(1)} %convert_element_type.193, bf16[10,256,768]{2,1,0:T(8,128)(2,1)} %param.24, bf16[10,5313,256]{2,1,0:T(8,128)(2,1)} %get-tuple-element.74, bf16[768,5313]{1,0:T(8,128)(2,1)} %all-gather.2.cloned.1.call-done), kind=kOutput, calls=%fused_computation.62 | convolution fusion | flops 20903362560 | bytes 51105280 | tf_op jit(solution)/shard_map/wtb,ct->wbc/dot_general | solution.py:162
  232.3 6.5 %multiply_reduce_fusion = (f32[384]{0:T(512)S(1)}, f32[384]{0:T(512)S(1)}, f32[10,256,384]{2,1,0:T(8,128)S(1)}) fusion(f32[10,256,384]{2,1,0:T(8,128)S(1)} %copy-done.9, f32[384]{0:T(512)S(1)} %copy-done.43, f32[384]{0:T(512)S(1)} %copy-done.32, bf16[10,256,768]{2,1,0:T(8,128)(2,1)} %get-tuple-element.72, bf16[768,384,1]{1,0,2:T(8,128)(2,1)S(1)} %bitcast.234), kind=kOutput, calls=%fused_computation.79 | convolution fusion | flops 1533541632 | bytes 12392448 | tf_op jit(solution)/shard_map/wbc,ch->wbh/dot_general | solution.py:168
  242.1 27.7 %bitcast_convert_fusion = bf16[768,5313]{0,1:T(8,128)(2,1)} fusion(bf16[10,256,768]{2,1,0:T(8,128)(2,1)} %fusion.35, bf16[10,5313,256]{2,1,0:T(8,128)(2,1)} %get-tuple-element.74), kind=kOutput, calls=%fused_computation.15 | convolution fusion | flops 20895645696 | bytes 39295488 | tf_op jit(solution)/shard_map/wbc,wtb->ct/dot_general | solution.py:158
  270.0 4.4 fusion.84
  277.3 11.2 %copy.80 = bf16[768,5313]{1,0:T(8,128)(2,1)} copy(bf16[768,5313]{0,1:T(8,128)(2,1)} %bitcast_convert_fusion) | data formatting | bytes 16321536 | tf_op jit(solution)/shard_map/convert_element_type | solution.py:160
  289.7 3.8 collective-permute-start.24
  295.9 4.7 dynamic-slice_bitcast_fusion
  312.6 3.9 convert_element_type.207
  322.6 5.4 %fusion.71 = f32[10,256,768]{2,1,0:T(8,128)} fusion(bf16[10,11,384]{2,1,0:T(8,128)(2,1)S(1)} %get-tuple-element.126, bf16[10,256,384]{2,1,0:T(8,128)(2,1)S(1)} %multiply_convert_fusion, bf16[3,768,384]{2,1,0:T(8,128)(2,1)S(1)} %copy-done.13), kind=kOutput, calls=%fused_computation.111 | convolution fusion | flops 1513881600 | bytes 10543104 | tf_op jit(solution)/shard_map/wbh,ch->wbc/dot_general | solution.py:228
  328.0 12.3 %fusion.45 = (f32[768]{0:T(1024)S(1)}, f32[768]{0:T(1024)S(1)}, f32[10,256,768]{2,1,0:T(8,128)}) fusion(bf16[10,256,768]{2,1,0:T(8,128)(2,1)S(1)} %copy-done.2, f32[768]{0:T(1024)S(1)} %copy-done.29, f32[768]{0:T(1024)S(1)} %copy-done.27, f32[768]{0:T(1024)S(1)} %copy-done.39, f32[768]{0:T(1024)S(1)} %copy-done.25, f32[10,256,768]{2,1,0:T(8,128)S(1)} %fusion.69, ...), kind=kOutput, calls=%fused_computation.61 | convolution fusion | flops 1566964224 | bytes 30099456 | tf_op jit(solution)/shard_map/wbh,ch->wbc/dot_general | solution.py:228
  340.8 3.2 fusion.19
  350.6 54.7 %collective-permute-done.27 = f32[2,768]{1,0:T(2,128)S(1)} collective-permute-done((f32[2,768]{1,0:T(2,128)S(1)}, f32[2,768]{1,0:T(2,128)S(1)}, u32[]{:S(2)}, u32[]{:S(2)}) %collective-permute-start.27) | collective-permute-done | bytes 6176 | tf_op jit(solution)/shard_map/ppermute | solution.py:25
  419.3 3.2 fusion.47
  422.7 9.5 %fusion.26 = f32[10,256,768]{2,1,0:T(8,128)} fusion(bf16[10,256,768]{2,1,0:T(8,128)(2,1)S(1)} %copy-done.3, f32[10,256,768]{2,1,0:T(8,128)} %get-tuple-element.145, f32[10,256,768]{2,1,0:T(8,128)} %get-tuple-element.143, bf16[10,256,768]{2,1,0:T(8,128)(2,1)S(1)} %copy-done.14, f32[768]{0:T(1024)S(1)} %get-tuple-element.39, f32[768]{0:T(1024)S(1)} %mul.822, ...), kind=kLoop, calls=%fused_computation.42 | loop fusion | flops 29491200 | bytes 31485952 | tf_op jit(solution)/shard_map/add | solution.py:248
  433.3 12.9 %collective-permute-done.38 = bf16[4,24,5313]{2,1,0:T(8,128)(2,1)S(1)} collective-permute-done((bf16[4,24,5313]{2,1,0:T(8,128)(2,1)S(1)}, bf16[4,24,5313]{2,1,0:T(8,128)(2,1)S(1)}, u32[]{:S(2)}, u32[]{:S(2)}) %collective-permute-start.38) | collective-permute-done | bytes 1020128 | tf_op jit(solution)/shard_map/ppermute | solution.py:25
  447.7 10.6 %collective-permute-done.39 = bf16[2,24,5313]{2,1,0:T(8,128)(2,1)S(1)} collective-permute-done((bf16[2,24,5313]{2,1,0:T(8,128)(2,1)S(1)}, bf16[2,24,5313]{2,1,0:T(8,128)(2,1)S(1)}, u32[]{:S(2)}, u32[]{:S(2)}) %collective-permute-start.39) | collective-permute-done | bytes 510080 | tf_op jit(solution)/shard_map/ppermute | solution.py:25
  459.9 9.4 %collective-permute-done.40 = bf16[1,24,5313]{2,1,0:T(8,128)(2,1)S(1)} collective-permute-done((bf16[1,24,5313]{2,1,0:T(8,128)(2,1)S(1)}, bf16[1,24,5313]{2,1,0:T(8,128)(2,1)S(1)}, u32[]{:S(2)}, u32[]{:S(2)}) %collective-permute-start.40) | collective-permute-done | bytes 255056 | tf_op jit(solution)/shard_map/ppermute | solution.py:25
  (284 shorter events, 103.2 us)
Async XLA Ops:
  7.2 121.9 %all-gather.2.cloned.1.call-start = ((), (), s32[]{:S(2)}) async-start(), calls=%async_computation | async-start | bytes 8515584 | tf_op jit(solution)/shard_map/all_gather | solution.py:124
  18.6 5.6 %collective-permute-start.3 = (f32[3,768]{1,0:T(4,128)S(1)}, f32[3,768]{1,0:T(4,128)S(1)}, u32[]{:S(2)}, u32[]{:S(2)}) collective-permute-start(f32[3,768]{1,0:T(4,128)S(1)} %pad_maximum_fusion.13), channel_id=1, source_target_pairs={{0,2},{1,3},{2,0},{3,1},{4,6},{5,7},{6,4},{7,5},{8,10},{9,11},{10,... | collective-permute-start | bytes 27656 | tf_op jit(solution)/shard_map/ppermute | solution.py:25
  21.5 9.6 %collective-permute-start.7 = (bf16[1,24,1536]{2,1,0:T(8,128)(2,1)S(1)}, bf16[1,24,1536]{2,1,0:T(8,128)(2,1)S(1)}, u32[]{:S(2)}, u32[]{:S(2)}) collective-permute-start(bf16[1,24,1536]{2,1,0:T(8,128)(2,1)S(1)} %maximum_bitcast_fusion.1), channel_id=1, source_target_pairs={{0,16},{4,20},{8,24},{12,28},{16,0},{20,4},{24,8},{28,12},{1,17},{... | collective-permute-start | bytes 221192 | tf_op jit(solution)/shard_map/ppermute | solution.py:25
  24.3 7.0 %collective-permute-start.4 = (f32[3,768]{1,0:T(4,128)S(1)}, f32[3,768]{1,0:T(4,128)S(1)}, u32[]{:S(2)}, u32[]{:S(2)}) collective-permute-start(f32[3,768]{1,0:T(4,128)S(1)} %pad_maximum_fusion.14), channel_id=1, source_target_pairs={{0,4},{4,0},{8,12},{12,8},{16,20},{20,16},{24,28},{28,24},{1,5},{5... | collective-permute-start | bytes 27656 | tf_op jit(solution)/shard_map/ppermute | solution.py:25
  31.2 5.9 %collective-permute-start.8 = (bf16[2,24,1536]{2,1,0:T(8,128)(2,1)S(1)}, bf16[2,24,1536]{2,1,0:T(8,128)(2,1)S(1)}, u32[]{:S(2)}, u32[]{:S(2)}) collective-permute-start(bf16[2,24,1536]{2,1,0:T(8,128)(2,1)S(1)} %maximum_bitcast_fusion), channel_id=1, source_target_pairs={{0,8},{4,12},{8,0},{12,4},{16,24},{20,28},{24,16},{28,20},{1,9},{5... | collective-permute-start | bytes 442376 | tf_op jit(solution)/shard_map/ppermute | solution.py:25
  31.4 11.3 %collective-permute-start.5 = (f32[3,768]{1,0:T(4,128)S(1)}, f32[3,768]{1,0:T(4,128)S(1)}, u32[]{:S(2)}, u32[]{:S(2)}) collective-permute-start(f32[3,768]{1,0:T(4,128)S(1)} %pad_maximum_fusion.15), channel_id=1, source_target_pairs={{0,8},{4,12},{8,0},{12,4},{16,24},{20,28},{24,16},{28,20},{1,9},{5... | collective-permute-start | bytes 27656 | tf_op jit(solution)/shard_map/ppermute | solution.py:25
  37.1 10.1 %collective-permute-start.9 = (bf16[4,24,1536]{2,1,0:T(8,128)(2,1)S(1)}, bf16[4,24,1536]{2,1,0:T(8,128)(2,1)S(1)}, u32[]{:S(2)}, u32[]{:S(2)}) collective-permute-start(bf16[4,24,1536]{2,1,0:T(8,128)(2,1)S(1)} %bitcast.232), channel_id=1, source_target_pairs={{0,4},{4,0},{8,12},{12,8},{16,20},{20,16},{24,28},{28,24},{1,5},{5... | collective-permute-start | bytes 884744 | tf_op jit(solution)/shard_map/ppermute | solution.py:25
  40.0 27.1 %collective-permute-start = (bf16[10,11,768]{2,1,0:T(8,128)(2,1)S(1)}, bf16[10,11,768]{2,1,0:T(8,128)(2,1)S(1)}, u32[]{:S(2)}, u32[]{:S(2)}) collective-permute-start(bf16[10,11,768]{2,1,0:T(8,128)(2,1)S(1)} %get-tuple-element.96), channel_id=1, source_target_pairs={{0,1},{1,2},{2,3},{4,5},{5,6},{6,7},{8,9},{9,10},{10,11},{12,13},{... | collective-permute-start | bytes 506888 | tf_op jit(solution)/shard_map/ppermute | solution.py:66
  41.3 25.8 %collective-permute-start.1 = (bf16[10,11,768]{2,1,0:T(8,128)(2,1)S(1)}, bf16[10,11,768]{2,1,0:T(8,128)(2,1)S(1)}, u32[]{:S(2)}, u32[]{:S(2)}) collective-permute-start(bf16[10,11,768]{2,1,0:T(8,128)(2,1)S(1)} %get-tuple-element.97), channel_id=1, source_target_pairs={{1,0},{2,1},{3,2},{5,4},{6,5},{7,6},{9,8},{10,9},{11,10},{13,12},{... | collective-permute-start | bytes 506888 | tf_op jit(solution)/shard_map/ppermute | solution.py:66
  47.5 19.2 %collective-permute-start.10 = (bf16[8,24,1536]{2,1,0:T(8,128)(2,1)S(1)}, bf16[8,24,1536]{2,1,0:T(8,128)(2,1)S(1)}, u32[]{:S(2)}, u32[]{:S(2)}) collective-permute-start(bf16[8,24,1536]{2,1,0:T(8,128)(2,1)S(1)} %bitcast.225), channel_id=1, source_target_pairs={{0,2},{1,3},{2,0},{3,1},{4,6},{5,7},{6,4},{7,5},{8,10},{9,11},{10,... | collective-permute-start | bytes 1769480 | tf_op jit(solution)/shard_map/ppermute | solution.py:25
  47.6 7.2 %collective-permute-start.6 = (f32[3,768]{1,0:T(4,128)S(1)}, f32[3,768]{1,0:T(4,128)S(1)}, u32[]{:S(2)}, u32[]{:S(2)}) collective-permute-start(f32[3,768]{1,0:T(4,128)S(1)} %pad_maximum_fusion.16), channel_id=1, source_target_pairs={{0,16},{4,20},{8,24},{12,28},{16,0},{20,4},{24,8},{28,12},{1,17},{... | collective-permute-start | bytes 27656 | tf_op jit(solution)/shard_map/ppermute | solution.py:25
  67.0 9.9 %collective-permute-start.11 = (bf16[16,24,1536]{2,1,0:T(8,128)(2,1)S(1)}, bf16[16,24,1536]{2,1,0:T(8,128)(2,1)S(1)}, u32[]{:S(2)}, u32[]{:S(2)}) collective-permute-start(bf16[16,24,1536]{2,1,0:T(8,128)(2,1)S(1)} %bitcast.218), channel_id=1, source_target_pairs={{0,1},{1,0},{2,3},{3,2},{4,5},{5,4},{6,7},{7,6},{8,9},{9,8},{10,11... | collective-permute-start | bytes 3538952 | tf_op jit(solution)/shard_map/ppermute | solution.py:25
  103.7 7.4 %collective-permute-start.14 = (f32[3,384]{1,0:T(4,128)S(1)}, f32[3,384]{1,0:T(4,128)S(1)}, u32[]{:S(2)}, u32[]{:S(2)}) collective-permute-start(f32[3,384]{1,0:T(4,128)S(1)} %pad_maximum_fusion.19), channel_id=1, source_target_pairs={{0,4},{4,0},{8,12},{12,8},{16,20},{20,16},{24,28},{28,24},{1,5},{5... | collective-permute-start | bytes 13832 | tf_op jit(solution)/shard_map/ppermute | solution.py:25
  105.8 133.1 %collective-permute-start.23 = (f32[10,11]{1,0:T(8,128)}, f32[10,11]{1,0:T(8,128)}, u32[]{:S(2)}, u32[]{:S(2)}) collective-permute-start(f32[10,11]{1,0:T(8,128)} %get-tuple-element.109), channel_id=1, source_target_pairs={{1,0},{2,1},{3,2},{5,4},{6,5},{7,6},{9,8},{10,9},{11,10},{13,12},{... | collective-permute-start | bytes 1328 | tf_op jit(solution)/shard_map/ppermute | solution.py:66
  107.1 10.4 %collective-permute-start.25 = (f32[10,11]{1,0:T(8,128)S(1)}, f32[10,11]{1,0:T(8,128)S(1)}, u32[]{:S(2)}, u32[]{:S(2)}) collective-permute-start(f32[10,11]{1,0:T(8,128)S(1)} %get-tuple-element.110), channel_id=1, source_target_pairs={{0,1},{1,2},{2,3},{4,5},{5,6},{6,7},{8,9},{9,10},{10,11},{12,13},{... | collective-permute-start | bytes 1328 | tf_op jit(solution)/shard_map/ppermute | solution.py:66
  240.9 28.8 %collective-permute-start.18 = (f32[6849]{0:T(1024)S(1)}, f32[6849]{0:T(1024)S(1)}, u32[]{:S(2)}, u32[]{:S(2)}) collective-permute-start(f32[6849]{0:T(1024)S(1)} %fusion.153), channel_id=1, source_target_pairs={{0,2},{1,3},{2,0},{3,1},{4,6},{5,7},{6,4},{7,5},{8,10},{9,11},{10,... | collective-permute-start | bytes 82196 | tf_op jit(solution)/shard_map/ppermute | solution.py:25
  274.4 19.1 %collective-permute-start.20 = (f32[6849]{0:T(1024)S(1)}, f32[6849]{0:T(1024)S(1)}, u32[]{:S(2)}, u32[]{:S(2)}) collective-permute-start(f32[6849]{0:T(1024)S(1)} %add.898), channel_id=1, source_target_pairs={{0,8},{4,12},{8,0},{12,4},{16,24},{20,28},{24,16},{28,20},{1,9},{5... | collective-permute-start | bytes 82196 | tf_op jit(solution)/shard_map/ppermute | solution.py:25
  288.4 30.5 %collective-permute-start.22 = (f32[10,11,768]{2,1,0:T(8,128)}, f32[10,11,768]{2,1,0:T(8,128)S(1)}, u32[]{:S(2)}, u32[]{:S(2)}) collective-permute-start(f32[10,11,768]{2,1,0:T(8,128)} %get-tuple-element.94), channel_id=1, source_target_pairs={{1,0},{2,1},{3,2},{5,4},{6,5},{7,6},{9,8},{10,9},{11,10},{13,12},{... | collective-permute-start | bytes 1013768 | tf_op jit(solution)/shard_map/ppermute | solution.py:66
  289.7 29.2 %collective-permute-start.24 = (f32[10,11,768]{2,1,0:T(8,128)S(1)}, f32[10,11,768]{2,1,0:T(8,128)}, u32[]{:S(2)}, u32[]{:S(2)}) collective-permute-start(f32[10,11,768]{2,1,0:T(8,128)S(1)} %get-tuple-element.95), channel_id=1, source_target_pairs={{0,1},{1,2},{2,3},{4,5},{5,6},{6,7},{8,9},{9,10},{10,11},{12,13},{... | collective-permute-start | bytes 1013768 | tf_op jit(solution)/shard_map/ppermute | solution.py:66
  293.6 7.0 %collective-permute-start.21 = (f32[6849]{0:T(1024)S(1)}, f32[6849]{0:T(1024)S(1)}, u32[]{:S(2)}, u32[]{:S(2)}) collective-permute-start(f32[6849]{0:T(1024)S(1)} %add.899), channel_id=1, source_target_pairs={{0,16},{4,20},{8,24},{12,28},{16,0},{20,4},{24,8},{28,12},{1,17},{... | collective-permute-start | bytes 82196 | tf_op jit(solution)/shard_map/ppermute | solution.py:25
  300.6 40.2 %collective-permute-start.36 = (bf16[16,24,5313]{2,1,0:T(8,128)(2,1)}, bf16[16,24,5313]{2,1,0:T(8,128)(2,1)}, u32[]{:S(2)}, u32[]{:S(2)}) collective-permute-start(bf16[16,24,5313]{2,1,0:T(8,128)(2,1)} %dynamic-slice_bitcast_fusion), channel_id=1, source_target_pairs={{0,1},{1,0},{2,3},{3,2},{4,5},{5,4},{6,7},{7,6},{8,9},{9,8},{10,11... | collective-permute-start | bytes 12241160 | tf_op jit(solution)/shard_map/ppermute | solution.py:25
  318.9 27.0 %collective-permute-start.31 = (bf16[16,24,1536]{2,1,0:T(8,128)(2,1)}, bf16[16,24,1536]{2,1,0:T(8,128)(2,1)}, u32[]{:S(2)}, u32[]{:S(2)}) collective-permute-start(bf16[16,24,1536]{2,1,0:T(8,128)(2,1)} %fusion.95), channel_id=1, source_target_pairs={{0,1},{1,0},{2,3},{3,2},{4,5},{5,4},{6,7},{7,6},{8,9},{9,8},{10,11... | collective-permute-start | bytes 3538952 | tf_op jit(solution)/shard_map/ppermute | solution.py:25
  340.3 9.0 %collective-permute-start.26 = (f32[2,768]{1,0:T(2,128)S(1)}, f32[2,768]{1,0:T(2,128)S(1)}, u32[]{:S(2)}, u32[]{:S(2)}) collective-permute-start(f32[2,768]{1,0:T(2,128)S(1)} %pad_maximum_fusion.22), channel_id=1, source_target_pairs={{0,1},{1,0},{2,3},{3,2},{4,5},{5,4},{6,7},{7,6},{8,9},{9,8},{10,11... | collective-permute-start | bytes 18440 | tf_op jit(solution)/shard_map/ppermute | solution.py:25
  345.5 73.8 %collective-permute-start.37 = (bf16[8,24,5313]{2,1,0:T(8,128)(2,1)}, bf16[8,24,5313]{2,1,0:T(8,128)(2,1)}, u32[]{:S(2)}, u32[]{:S(2)}) collective-permute-start(bf16[8,24,5313]{2,1,0:T(8,128)(2,1)} %dynamic-slice_bitcast_fusion.1), channel_id=1, source_target_pairs={{0,2},{1,3},{2,0},{3,1},{4,6},{5,7},{6,4},{7,5},{8,10},{9,11},{10,... | collective-permute-start | bytes 6120584 | tf_op jit(solution)/shard_map/ppermute | solution.py:25
  348.5 68.9 %collective-permute-start.32 = (bf16[8,24,1536]{2,1,0:T(8,128)(2,1)S(1)}, bf16[8,24,1536]{2,1,0:T(8,128)(2,1)S(1)}, u32[]{:S(2)}, u32[]{:S(2)}) collective-permute-start(bf16[8,24,1536]{2,1,0:T(8,128)(2,1)S(1)} %dynamic-slice_bitcast_fusion.3), channel_id=1, source_target_pairs={{0,2},{1,3},{2,0},{3,1},{4,6},{5,7},{6,4},{7,5},{8,10},{9,11},{10,... | collective-permute-start | bytes 1769480 | tf_op jit(solution)/shard_map/ppermute | solution.py:25
  349.3 56.1 %collective-permute-start.27 = (f32[2,768]{1,0:T(2,128)S(1)}, f32[2,768]{1,0:T(2,128)S(1)}, u32[]{:S(2)}, u32[]{:S(2)}) collective-permute-start(f32[2,768]{1,0:T(2,128)S(1)} %fusion.133), channel_id=1, source_target_pairs={{0,2},{1,3},{2,0},{3,1},{4,6},{5,7},{6,4},{7,5},{8,10},{9,11},{10,... | collective-permute-start | bytes 18440 | tf_op jit(solution)/shard_map/ppermute | solution.py:25
  417.6 14.7 %collective-permute-start.33 = (bf16[4,24,1536]{2,1,0:T(8,128)(2,1)S(1)}, bf16[4,24,1536]{2,1,0:T(8,128)(2,1)S(1)}, u32[]{:S(2)}, u32[]{:S(2)}) collective-permute-start(bf16[4,24,1536]{2,1,0:T(8,128)(2,1)S(1)} %dynamic-slice_bitcast_fusion.5), channel_id=1, source_target_pairs={{0,4},{4,0},{8,12},{12,8},{16,20},{20,16},{24,28},{28,24},{1,5},{5... | collective-permute-start | bytes 884744 | tf_op jit(solution)/shard_map/ppermute | solution.py:25
  422.6 23.5 %collective-permute-start.38 = (bf16[4,24,5313]{2,1,0:T(8,128)(2,1)S(1)}, bf16[4,24,5313]{2,1,0:T(8,128)(2,1)S(1)}, u32[]{:S(2)}, u32[]{:S(2)}) collective-permute-start(bf16[4,24,5313]{2,1,0:T(8,128)(2,1)S(1)} %dynamic-slice_bitcast_fusion.2), channel_id=1, source_target_pairs={{0,4},{4,0},{8,12},{12,8},{16,20},{20,16},{24,28},{28,24},{1,5},{5... | collective-permute-start | bytes 3060296 | tf_op jit(solution)/shard_map/ppermute | solution.py:25
  432.4 14.7 %collective-permute-start.34 = (bf16[2,24,1536]{2,1,0:T(8,128)(2,1)S(1)}, bf16[2,24,1536]{2,1,0:T(8,128)(2,1)S(1)}, u32[]{:S(2)}, u32[]{:S(2)}) collective-permute-start(bf16[2,24,1536]{2,1,0:T(8,128)(2,1)S(1)} %dynamic-slice_bitcast_fusion.6), channel_id=1, source_target_pairs={{0,8},{4,12},{8,0},{12,4},{16,24},{20,28},{24,16},{28,20},{1,9},{5... | collective-permute-start | bytes 442376 | tf_op jit(solution)/shard_map/ppermute | solution.py:25
  446.4 11.9 %collective-permute-start.39 = (bf16[2,24,5313]{2,1,0:T(8,128)(2,1)S(1)}, bf16[2,24,5313]{2,1,0:T(8,128)(2,1)S(1)}, u32[]{:S(2)}, u32[]{:S(2)}) collective-permute-start(bf16[2,24,5313]{2,1,0:T(8,128)(2,1)S(1)} %dynamic-slice_bitcast_fusion.4), channel_id=1, source_target_pairs={{0,8},{4,12},{8,0},{12,4},{16,24},{20,28},{24,16},{28,20},{1,9},{5... | collective-permute-start | bytes 1530152 | tf_op jit(solution)/shard_map/ppermute | solution.py:25
  447.1 11.4 %collective-permute-start.35 = (bf16[1,24,1536]{2,1,0:T(8,128)(2,1)S(1)}, bf16[1,24,1536]{2,1,0:T(8,128)(2,1)S(1)}, u32[]{:S(2)}, u32[]{:S(2)}) collective-permute-start(bf16[1,24,1536]{2,1,0:T(8,128)(2,1)S(1)} %constant_dynamic-slice_fusion.1), channel_id=1, source_target_pairs={{0,16},{4,20},{8,24},{12,28},{16,0},{20,4},{24,8},{28,12},{1,17},{... | collective-permute-start | bytes 221192 | tf_op jit(solution)/shard_map/ppermute | solution.py:25
  458.5 10.9 %collective-permute-start.40 = (bf16[1,24,5313]{2,1,0:T(8,128)(2,1)S(1)}, bf16[1,24,5313]{2,1,0:T(8,128)(2,1)S(1)}, u32[]{:S(2)}, u32[]{:S(2)}) collective-permute-start(bf16[1,24,5313]{2,1,0:T(8,128)(2,1)S(1)} %constant_dynamic-slice_fusion), channel_id=1, source_target_pairs={{0,16},{4,20},{8,24},{12,28},{16,0},{20,4},{24,8},{28,12},{1,17},{... | collective-permute-start | bytes 765080 | tf_op jit(solution)/shard_map/ppermute | solution.py:25
  (60 other events, 571.7 us)
Sparse Core Ops, SparseCore 0:
  10.9 84.6 all-gather.1
